TPU v7x, 32 devices: a whole 2x2x4 slice. The times are simulated.
32 devices in a mesh: row: 4 (over y, core), col: 8 (over z, x).
Axes of the slice: x: 2, y: 2, z: 4, core: 2. Of those that a mesh axis runs over, the one named last changes fastest.
Arguments:
- ainv_top: float32 [4096, 4096], P('row', 'col'), may hold values from -0.25 to 0.25
- par_struct: int32 [8, 16], replicated, may hold values from 0 to 31, as said below
- par_panel: float32 [8, 16, 128, 128], P('col', 'row'), may hold values from -6 to 6
- par_linv: float32 [8, 128, 128], P('col', 'row'), may hold values from -0.0625 to 0.0625
- par_dinv: float32 [8, 128, 128], P('col', 'row'), may hold values from -192 to 192
- kid_panel: float32 [16, 16, 128, 128], P('col', 'row'), may hold values from -6 to 6
- kid_upper: float32 [16, 128, 128], P('col', 'row'), may hold values from -6 to 6
- kid_linv: float32 [16, 128, 128], P('col', 'row'), may hold values from -0.0625 to 0.0625
- kid_dinv: float32 [16, 128, 128], P('col', 'row'), may hold values from -192 to 192
Outputs:
- par_offdiag: float32 [8, 16, 128, 128], P('col', 'row')
- par_diag: float32 [8, 128, 128], P('col', 'row')
- kid_offdiag: float32 [16, 16, 128, 128], P('col', 'row')
- kid_parent: float32 [16, 128, 128], P('col', 'row')
- kid_diag: float32 [16, 128, 128], P('col', 'row')
Inputs may be any that keep to these rules, and one draw needn't show every extreme that they name: `par_struct`: in every row, entries 2j and 2j + 1 are two different ancestors among j * 4 to (j + 1) * 4 - 1.
All inputs are finite; a program needn't handle non-finite values.
Results may differ from a plain program's by a relative error of at most 0.00014.
Values sent between devices are 32-bit elements; how exact they have to be, the bound alone decides.
No kernel may reach another device: no remote copies, remote signals or barrier semaphores. Data moves between devices by JAX's collectives and lax.ppermute only.
A program may use at most 128 MiB of HBM per device.

v0:
```python
import jax
import jax.numpy as jnp
from jax import lax
from jax.sharding import PartitionSpec as P

high = lax.Precision.HIGH
highest = lax.Precision.HIGHEST


def mm(spec, *operands, precision=high):
    return jnp.einsum(spec, *operands, precision=precision)


def on_device(
    ainv_top, par_struct, par_panel, par_linv, par_dinv, kid_panel, kid_upper, kid_linv, kid_dinv
):
    grid_rows = lax.axis_size("row")
    grid_cols = lax.axis_size("col")
    my_row = lax.axis_index("row")
    my_col = lax.axis_index("col")
    width = par_panel.shape[-1]
    band_rows = width // grid_rows
    slot_share = par_panel.shape[1]
    children = kid_panel.shape[0]
    pair_width = par_struct.shape[1] // grid_cols
    tile_rows = ainv_top.shape[0] // width
    tile_cols = ainv_top.shape[1] // width
    local_tiles = ainv_top.reshape(tile_rows, width, tile_cols, width)
    pick_rows = lax.dynamic_slice_in_dim(par_struct, my_row * slot_share, slot_share, 1)
    pick_cols = lax.dynamic_slice_in_dim(par_struct, my_col * pair_width, pair_width, 1)
    pick_rows = pick_rows - my_row * tile_rows
    pick_cols = pick_cols - my_col * tile_cols
    tiles = local_tiles[pick_rows[:, :, None], :, pick_cols[:, None, :], :]
    small = jnp.concatenate([par_linv, par_dinv, kid_upper, kid_linv, kid_dinv], axis=0)
    small = lax.all_gather(small, "row", axis=1, tiled=True)
    plinv, pdinv = (small[0], small[1])
    kupper = small[2 : 2 + children]
    klinv = small[2 + children : 2 + 2 * children]
    kdinv = small[2 + 2 * children :]
    panels = jnp.concatenate([par_panel, kid_panel], axis=0)
    every = lax.all_gather(panels, "row", axis=1, tiled=True)
    moved = lax.all_to_all(tiles, "col", 0, 0, tiled=True)
    every = every.reshape(1 + children, grid_cols, pair_width, width, width)
    prod = mm("cjkab,nckbd->njad", moved, every)
    par_off = -mm("jab,bc->jac", prod[0], plinv)
    par_hat = mm("jab,bc->jac", par_panel[0], plinv)
    kid_hat = mm("njab,nbc->njac", kid_panel, klinv)
    kuphat = mm("nab,nbc->nac", kupper, klinv)
    kid_sum = prod[1:] + mm("jab,nbc->njac", par_off, kupper)
    kid_off = -mm("njab,nbc->njac", kid_sum, klinv)
    diag_part = mm("jba,jbc->ac", par_hat, par_off)
    parent_part = mm("jba,njbc->nac", par_off, kid_hat)
    hat_part = mm("njba,njbc->nac", kid_hat, kid_off)
    inner = parent_part - mm("ab,nbc->nac", diag_part, kuphat)
    edge_part = mm("nba,nbc->nac", kuphat, inner) - hat_part
    parts = jnp.concatenate([diag_part[None], parent_part, edge_part], axis=0)
    parts = parts.reshape(1 + 2 * children, grid_rows, band_rows, width)
    parts = lax.all_to_all(parts, "row", 1, 1, tiled=True)
    sums = parts.sum(axis=1)
    par_pivot = mm("ba,bc,cd->ad", plinv, pdinv, plinv)
    kid_pivot = mm("nba,nbc,ncd->nad", klinv, kdinv, klinv)
    kid_pivot = kid_pivot + mm("nba,bc,ncd->nad", kuphat, par_pivot, kuphat)
    start = my_row * band_rows
    par_diag = lax.dynamic_slice_in_dim(par_pivot, start, band_rows, 0) - sums[0]
    kid_par = -(sums[1 : 1 + children] + mm("ab,nbc->nac", par_diag, kuphat))
    kid_diag = lax.dynamic_slice_in_dim(kid_pivot, start, band_rows, 1) + sums[1 + children :]
    return (par_off[None], par_diag[None], kid_off, kid_par, kid_diag)


def solution(mesh):
    placed = (
        P("row", "col"),
        P(),
        P("col", "row", None, None),
        P("col", "row", None),
        P("col", "row", None),
        P("col", "row", None, None),
        P("col", "row", None),
        P("col", "row", None),
        P("col", "row", None),
    )
    return jax.shard_map(
        on_device,
        mesh=mesh,
        in_specs=placed,
        out_specs=(
            P("col", "row", None, None),
            P("col", "row", None),
            P("col", "row", None, None),
            P("col", "row", None),
            P("col", "row", None),
        ),
        check_vma=False,
    )
```

profile of v0, /device:TPU:0, one launch (start us, length us, event | category | flops | bytes accessed | tf_op | source)
XLA Modules:
  0.0 147.9 jit_solution(1128994719983951276)
XLA Ops:
  7.2 0.8 fusion.41
  7.9 0.8 fusion.43
  8.9 2.9 %reshape.58 = f32[8,128,4,128]{3,2,1,0:T(4,128)} reshape(f32[1024,512]{1,0:T(8,128)} %param.9) | data formatting | bytes 4194304 | tf_op jit(solution)/shard_map/reshape | solution.py:28
  11.8 1.9 %copy.49 = f32[8,128,4,128]{3,1,2,0:T(8,128)S(1)} copy(f32[8,128,4,128]{3,2,1,0:T(4,128)} %reshape.58) | data formatting | bytes 4194304 | tf_op jit(solution)/shard_map/reshape | solution.py:28
  13.7 2.9 %gather_fusion = f32[64,128,128]{2,1,0:T(8,128)} fusion(f32[8,128,4,128]{3,1,2,0:T(8,128)S(1)} %copy.49, s32[64]{0:T(128)S(1)} %reshape.36), kind=kCustom, calls=%fused_computation | custom fusion | bytes 8389120 | tf_op jit(solution)/shard_map/gather | solution.py:33
  16.6 7.4 %all-to-all-start = ((f32[8,4,2,128,128]{4,3,2,1,0:T(8,128)}), f32[8,4,2,128,128]{4,3,2,1,0:T(8,128)}, u32[]{:S(2)}, u32[]{:S(2)}) async-start(f32[8,4,2,128,128]{4,3,2,1,0:T(8,128)} %bitcast.134), calls=%async_computation | async-start | bytes 8388608 | tf_op jit(solution)/shard_map/all_to_all | solution.py:42
  24.0 1.0 pad_maximum_fusion
  25.1 7.2 %all_gather.7 = f32[8,128,128]{2,1,0:T(8,128)S(1)} all-gather(f32[8,32,128]{2,1,0:T(8,128)S(1)} %constant_dynamic-update-slice_fusion), channel_id=1, replica_groups=mesh['row'=4,'col'=8] {'row'}, dimensions={1}, use_global_device_ids=true | all-gather | bytes 655360 | tf_op jit(solution)/shard_map/all_gather | solution.py:35
  32.3 0.3 fusion.24
  32.6 0.2 fusion.30
  32.8 0.2 fusion.21
  33.0 0.3 fusion.25
  33.3 0.3 convolution_bitcast_fusion.2
  33.7 0.3 fusion.17
  34.0 0.4 convolution_bitcast_fusion.1
  34.4 22.1 %all-gather.2.cloned.1.call-done = f32[3,16,128,128]{3,2,1,0:T(8,128)} async-done(((f32[3,4,128,128]{3,2,1,0:T(8,128)}), f32[3,16,128,128]{3,2,1,0:T(8,128)}) %all-gather.2.cloned.1.call-update) | async-done | bytes 3145744 | tf_op jit(solution)/shard_map/all_gather | solution.py:41
  56.5 60.8 %all-to-all-done = f32[8,4,2,128,128]{4,3,2,1,0:T(8,128)} async-done(((f32[8,4,2,128,128]{4,3,2,1,0:T(8,128)}), f32[8,4,2,128,128]{4,3,2,1,0:T(8,128)}, u32[]{:S(2)}, u32[]{:S(2)}) %all-to-all-start) | async-done | bytes 4194336 | tf_op jit(solution)/shard_map/all_to_all | solution.py:42
  117.3 7.8 %fusion.3 = f32[3,4,128,128]{2,3,1,0:T(8,128)S(1)} fusion(f32[3,8,2,128,128,1]{4,3,2,1,5,0:T(8,128)} %bitcast.136, f32[8,4,2,128,128]{4,3,2,1,0:T(8,128)} %all-to-all-done), kind=kOutput, calls=%fused_computation.4 | convolution fusion | flops 2415919104 | bytes 8126464 | tf_op jit(solution)/shard_map/cjkab,nckbd->njad/dot_general | solution.py:11
  125.1 0.4 convolution_negate_fusion.1
  125.5 0.4 fusion.6
  126.0 0.4 fusion.11
  126.3 0.3 fusion.45
  126.6 0.6 convolution_negate_fusion
  127.2 0.4 convolution_bitcast_fusion.3
  127.6 0.2 fusion.7
  127.8 0.3 convolution_subtract_fusion
  128.1 0.7 pad_maximum_fusion.1
  128.8 3.5 %all-to-all-start.1 = ((f32[5,4,32,128]{3,2,0,1:T(8,128)}), f32[5,4,32,128]{3,2,0,1:T(8,128)S(1)}, u32[]{:S(2)}, u32[]{:S(2)}) async-start(f32[5,4,32,128]{3,2,0,1:T(8,128)} %pad_maximum_fusion.1), calls=%async_computation.1 | async-start | bytes 655360 | tf_op jit(solution)/shard_map/all_to_all | solution.py:58
  132.7 6.3 %all-to-all-done.1 = f32[5,4,32,128]{3,2,0,1:T(8,128)S(1)} async-done(((f32[5,4,32,128]{3,2,0,1:T(8,128)}), f32[5,4,32,128]{3,2,0,1:T(8,128)S(1)}, u32[]{:S(2)}, u32[]{:S(2)}) %all-to-all-start.1) | async-done | bytes 327712 | tf_op jit(solution)/shard_map/all_to_all | solution.py:58
  139.0 0.8 fusion.9
  139.8 0.6 fusion.39
  140.4 0.6 slice_add_fusion
  (30 shorter events, 0.7 us)
Async XLA Ops:
  16.5 7.5 %copy-start.1 = (f32[2,4,128,128]{3,2,1,0:T(8,128)S(1)}, f32[2,4,128,128]{3,2,1,0:T(8,128)}, u32[]{:S(2)}) copy-start(f32[2,4,128,128]{3,2,1,0:T(8,128)} %param.14) | copy-start | bytes 1572868
  16.5 7.5 %copy-start.3 = (f32[1,4,128,128]{3,2,1,0:T(8,128)S(1)}, f32[1,4,128,128]{3,2,1,0:T(8,128)}, u32[]{:S(2)}) copy-start(f32[1,4,128,128]{3,2,1,0:T(8,128)} %param.11) | copy-start | bytes 786436
  16.5 8.5 %copy-start.7 = (f32[1,32,128]{2,1,0:T(8,128)S(1)}, f32[1,32,128]{2,1,0:T(8,128)}, u32[]{:S(2)}) copy-start(f32[1,32,128]{2,1,0:T(8,128)} %param.12) | copy-start | bytes 49156
  16.5 8.5 %copy-start.8 = (f32[1,32,128]{2,1,0:T(8,128)S(1)}, f32[1,32,128]{2,1,0:T(8,128)}, u32[]{:S(2)}) copy-start(f32[1,32,128]{2,1,0:T(8,128)} %param.13) | copy-start | bytes 49156
  16.5 8.5 %copy-start.4 = (f32[2,32,128]{2,1,0:T(8,128)S(1)}, f32[2,32,128]{2,1,0:T(8,128)}, u32[]{:S(2)}) copy-start(f32[2,32,128]{2,1,0:T(8,128)} %param.15) | copy-start | bytes 98308
  16.6 8.5 %copy-start.5 = (f32[2,32,128]{2,1,0:T(8,128)S(1)}, f32[2,32,128]{2,1,0:T(8,128)}, u32[]{:S(2)}) copy-start(f32[2,32,128]{2,1,0:T(8,128)} %param.16) | copy-start | bytes 98308
  16.6 8.5 %copy-start.6 = (f32[2,32,128]{2,1,0:T(8,128)S(1)}, f32[2,32,128]{2,1,0:T(8,128)}, u32[]{:S(2)}) copy-start(f32[2,32,128]{2,1,0:T(8,128)} %param.17) | copy-start | bytes 98308
  16.6 100.7 %all-to-all-start = ((f32[8,4,2,128,128]{4,3,2,1,0:T(8,128)}), f32[8,4,2,128,128]{4,3,2,1,0:T(8,128)}, u32[]{:S(2)}, u32[]{:S(2)}) async-start(f32[8,4,2,128,128]{4,3,2,1,0:T(8,128)} %bitcast.134), calls=%async_computation | async-start | bytes 8388608 | tf_op jit(solution)/shard_map/all_to_all | solution.py:42
  24.0 32.5 %all-gather.2.cloned.1.call-start = ((), (), s32[]{:S(2)}) async-start(), calls=%async_computation.2 | async-start | bytes 3932160 | tf_op jit(solution)/shard_map/all_gather | solution.py:41
  125.5 7.2 %copy-start = (f32[4,128,128]{2,1,0:T(8,128)}, f32[4,128,128]{2,1,0:T(8,128)S(1)}, u32[]{:S(2)}) copy-start(f32[4,128,128]{2,1,0:T(8,128)S(1)} %convolution_negate_fusion.1) | copy-start | bytes 786436
  127.2 13.8 %copy-start.2 = (f32[2,4,128,128]{3,2,1,0:T(8,128)}, f32[2,4,128,128]{3,2,1,0:T(8,128)S(1)}, u32[]{:S(2)}) copy-start(f32[2,4,128,128]{3,2,1,0:T(8,128)S(1)} %convolution_negate_fusion) | copy-start | bytes 1572868
  128.8 10.2 %all-to-all-start.1 = ((f32[5,4,32,128]{3,2,0,1:T(8,128)}), f32[5,4,32,128]{3,2,0,1:T(8,128)S(1)}, u32[]{:S(2)}, u32[]{:S(2)}) async-start(f32[5,4,32,128]{3,2,0,1:T(8,128)} %pad_maximum_fusion.1), calls=%async_computation.1 | async-start | bytes 655360 | tf_op jit(solution)/shard_map/all_to_all | solution.py:58
Sparse Core Ops, SparseCore 0:
  26.4 30.0 all-gather.1
where the time goes:
time: 148 us
  waiting for transfers between devices  89.2 us (60%)
  between operations  14.3 us (10%)
  matrix products  13.9 us (9%)
  starting transfers between devices  10.9 us (7%)
  local copies, waits for them, and re-layouts  7.82 us (5%)
  blocking collectives  7.2 us (5%)
  other arithmetic  4.55 us (3%)
    all_to_all x1, waiting for transfers between devices, on_device(): moved = lax.all_to_all(tiles, 'col', 0, 0, tiled=True)  60.8 us
    all_gather x1, waiting for transfers between devices, on_device(): every = lax.all_gather(panels, 'row', axis=1, tiled=True)  22.1 us
    dot_general x19, matrix products, mm(): return jnp.einsum(spec, *operands, precision=precision)  13.9 us
    all_to_all x1, starting transfers between devices, on_device(): moved = lax.all_to_all(tiles, 'col', 0, 0, tiled=True)  7.4 us
    all_gather x1, blocking collectives, on_device(): small = lax.all_gather(small, 'row', axis=1, tiled=True)  7.2 us
    all_to_all x1, waiting for transfers between devices, on_device(): parts = lax.all_to_all(parts, 'row', 1, 1, tiled=True)  6.27 us
    reshape x2, local copies, waits for them, and re-layouts, on_device(): local_tiles = ainv_top.reshape(tile_rows, width, tile_cols, width)  4.78 us
    all_to_all x1, starting transfers between devices, on_device(): parts = lax.all_to_all(parts, 'row', 1, 1, tiled=True)  3.45 us
  transfers between devices with their start and end apart: 3, of which 3 were waited for; matrix products, arithmetic and copies ran while one was open for 2% of the time, Pallas kernels for 0%

commit v1 on v0

--- a/solution.py
+++ b/solution.py
@@ -2,6 +2,7 @@
 import jax.numpy as jnp
 from jax import lax
 from jax.sharding import PartitionSpec as P
+from jax.lax import axis_index, ppermute, psum
 
 high = lax.Precision.HIGH
 highest = lax.Precision.HIGHEST
@@ -38,7 +39,19 @@
     klinv = small[2 + children : 2 + 2 * children]
     kdinv = small[2 + 2 * children :]
     panels = jnp.concatenate([par_panel, kid_panel], axis=0)
-    every = lax.all_gather(panels, "row", axis=1, tiled=True)
+    count_all = psum(1, axis_name="row")
+    seen = tuple(((t, (t + 1) % count_all) for t in range(count_all)))
+    samples = tuple(((t, (t - 1) % count_all) for t in range(count_all)))
+    work_now, big = ([panels], [panels])
+    for _ in range(count_all // 2):
+        frame_out = ppermute(work_now[-1], axis_name="row", perm=seen)
+        work_now.append(frame_out)
+    for _ in [*range((count_all - 1) // 2)]:
+        x_new = ppermute(big[-1], perm=samples, axis_name="row")
+        big.append(x_new)
+    fresh = jnp.concatenate([*work_now[::-1], *big[1:]], axis=1)
+    r_now = axis_index("row")
+    every = jnp.roll(fresh, shift=(r_now - count_all // 2) * panels.shape[1], axis=1)
     moved = lax.all_to_all(tiles, "col", 0, 0, tiled=True)
     every = every.reshape(1 + children, grid_cols, pair_width, width, width)
     prod = mm("cjkab,nckbd->njad", moved, every)

time: 148 us -> 133 us (0.90)
  waiting for transfers between devices: 89.2 us -> 65.8 us
  blocking collectives: 7.2 us -> 21.9 us
  between operations: 14.3 us -> 1.08 us
  local copies, waits for them, and re-layouts: 7.82 us -> 12.3 us
  other arithmetic: 4.55 us -> 2.26 us
  matrix products: 13.9 us -> 16.1 us
  starting transfers between devices: 10.9 us -> 13 us
    all_gather x1 -> x0, waiting for transfers between devices: 22.1 us -> none  [on_device(): every = lax.all_gather(panels, 'row', axis=1, tiled=True)]
    all_gather x1, blocking collectives: 7.2 us -> 21.9 us  [on_device(): small = lax.all_gather(small, 'row', axis=1, tiled=True)]
    all_to_all x1, waiting for transfers between devices: 60.8 us -> 52.6 us  [on_device(): moved = lax.all_to_all(tiles, 'col', 0, 0, tiled=True)]
    ppermute x0 -> x3, waiting for transfers between devices: none -> 7.84 us  [the longest x2 7.84 us: on_device(): frame_out = ppermute(work_now[-1], axis_name='row', perm=seen)]
    unnamed x22 -> x48, local copies, waits for them, and re-layouts: 0.06 us -> 3.47 us
    dot_general x19, matrix products: 13.9 us -> 16.1 us  [mm(): return jnp.einsum(spec, *operands, precision=precision)]
    ppermute x0 -> x3, starting transfers between devices: none -> 2.15 us  [the longest x1 1.74 us: on_device(): x_new = ppermute(big[-1], perm=samples, axis_name='row')]
  transfers between devices with their start and end apart: 3 -> 5, of which waited for: 3 -> 3; matrix products, arithmetic and copies ran while one was open for 2% -> 7% of each run, Pallas kernels for 0% -> 0%
where the time goes in v1:
time: 133 us; the launch traced here: 132 us
  waiting for transfers between devices  65.8 us (49%)
  blocking collectives  21.9 us (16%)
  matrix products  16.1 us (12%)
  starting transfers between devices  13 us (10%)
  local copies, waits for them, and re-layouts  12.3 us (9%)
  other arithmetic  2.26 us (2%)
    all_to_all x1, waiting for transfers between devices, on_device(): moved = lax.all_to_all(tiles, 'col', 0, 0, tiled=True)  52.6 us
    all_gather x1, blocking collectives, on_device(): small = lax.all_gather(small, 'row', axis=1, tiled=True)  21.9 us
    dot_general x19, matrix products, mm(): return jnp.einsum(spec, *operands, precision=precision)  16.1 us
    ppermute x2, waiting for transfers between devices, on_device(): frame_out = ppermute(work_now[-1], axis_name='row', perm=seen)  7.84 us
    all_to_all x1, starting transfers between devices, on_device(): moved = lax.all_to_all(tiles, 'col', 0, 0, tiled=True)  7.4 us
    all_to_all x1, waiting for transfers between devices, on_device(): parts = lax.all_to_all(parts, 'row', 1, 1, tiled=True)  5.36 us
    reshape x2, local copies, waits for them, and re-layouts, on_device(): local_tiles = ainv_top.reshape(tile_rows, width, tile_cols, width)  4.76 us
    unnamed x48, local copies, waits for them, and re-layouts  3.47 us
  transfers between devices with their start and end apart: 5, of which 3 were waited for; matrix products, arithmetic and copies ran while one was open for 7% of the time, Pallas kernels for 0%

profile of v1, /device:TPU:0, one launch (start us, length us, event | category | flops | bytes accessed | tf_op | source)
XLA Modules:
  0.0 132.4 jit_solution(9494493006125588796)
XLA Ops:
  0.6 2.9 %reshape.58 = f32[8,128,4,128]{3,2,1,0:T(4,128)} reshape(f32[1024,512]{1,0:T(8,128)} %param.9) | data formatting | bytes 4194304 | tf_op jit(solution)/shard_map/reshape | solution.py:29
  3.5 1.9 %copy.49 = f32[8,128,4,128]{3,1,2,0:T(8,128)S(1)} copy(f32[8,128,4,128]{3,2,1,0:T(4,128)} %reshape.58) | data formatting | bytes 4194304 | tf_op jit(solution)/shard_map/reshape | solution.py:29
  5.8 2.9 %gather_fusion = f32[64,128,128]{2,1,0:T(8,128)} fusion(f32[8,128,4,128]{3,1,2,0:T(8,128)S(1)} %copy.49, s32[64]{0:T(128)S(1)} %reshape.36), kind=kCustom, calls=%fused_computation | custom fusion | bytes 8389120 | tf_op jit(solution)/shard_map/gather | solution.py:34
  8.7 7.4 %all-to-all-start = ((f32[8,4,2,128,128]{4,3,2,1,0:T(8,128)}), f32[8,4,2,128,128]{4,3,2,1,0:T(8,128)}, u32[]{:S(2)}, u32[]{:S(2)}) async-start(f32[8,4,2,128,128]{4,3,2,1,0:T(8,128)} %bitcast.131), calls=%async_computation | async-start | bytes 8388608 | tf_op jit(solution)/shard_map/all_to_all | solution.py:55
  16.1 0.7 constant_dynamic-update-slice_fusion.1
  16.8 0.8 constant_dynamic-update-slice_fusion
  17.6 1.7 %collective-permute-start.2 = (f32[3,4,128,128]{3,2,1,0:T(8,128)}, f32[3,4,128,128]{3,2,1,0:T(8,128)S(1)}, u32[]{:S(2)}, u32[]{:S(2)}) collective-permute-start(f32[3,4,128,128]{3,2,1,0:T(8,128)} %constant_dynamic-update-slice_fusion), channel_id=1, source_target_pairs={{0,24},{8,0},{16,8},{24,16},{1,25},{9,1},{17,9},{25,17},{2,26},{10... | collective-permute-start | bytes 2359304 | tf_op jit(solution)/shard_map/ppermute | solution.py:50
  19.5 21.9 %all_gather.3 = f32[8,128,128]{2,1,0:T(8,128)S(1)} all-gather(f32[8,32,128]{2,1,0:T(8,128)S(1)} %constant_dynamic-update-slice_fusion.12), channel_id=1, replica_groups=mesh['row'=4,'col'=8] {'row'}, dimensions={1}, use_global_device_ids=true | all-gather | bytes 655360 | tf_op jit(solution)/shard_map/all_gather | solution.py:36
  41.6 0.3 convolution_bitcast_fusion.2
  42.2 0.4 collective-permute-start.1
  42.8 0.9 fusion.16
  43.8 0.9 fusion.24
  44.7 1.2 convolution_bitcast_fusion.1
  45.9 7.8 %collective-permute-done.1 = f32[3,4,128,128]{3,2,1,0:T(8,128)} collective-permute-done((f32[3,4,128,128]{3,2,1,0:T(8,128)S(1)}, f32[3,4,128,128]{3,2,1,0:T(8,128)}, u32[]{:S(2)}, u32[]{:S(2)}) %collective-permute-start.1) | collective-permute-done | bytes 786464 | tf_op jit(solution)/shard_map/ppermute | solution.py:47
  53.7 1.2 constant_dynamic-update-slice_fusion.11
  55.1 1.2 constant_dynamic-update-slice_fusion.6
  56.8 52.6 %all-to-all-done = f32[8,4,2,128,128]{4,3,2,1,0:T(8,128)} async-done(((f32[8,4,2,128,128]{4,3,2,1,0:T(8,128)}), f32[8,4,2,128,128]{4,3,2,1,0:T(8,128)}, u32[]{:S(2)}, u32[]{:S(2)}) %all-to-all-start) | async-done | bytes 4194336 | tf_op jit(solution)/shard_map/all_to_all | solution.py:55
  109.4 7.0 %fusion.3 = f32[3,4,128,128]{2,3,1,0:T(8,128)S(1)} fusion(f32[3,8,2,128,128,1]{4,3,2,1,5,0:T(8,128)S(1)} %bitcast.132, f32[8,4,2,128,128]{4,3,2,1,0:T(8,128)} %all-to-all-done), kind=kOutput, calls=%fused_computation.4 | convolution fusion | flops 2415919104 | bytes 8126464 | tf_op jit(solution)/shard_map/cjkab,nckbd->njad/dot_general | solution.py:12
  116.4 0.4 convolution_negate_fusion.1
  116.8 0.4 convolution_bitcast_fusion
  117.3 0.3 fusion.44
  117.5 0.4 fusion.10
  117.9 0.6 convolution_negate_fusion
  118.6 0.4 convolution_bitcast_fusion.3
  119.2 0.3 convolution_subtract_fusion
  119.5 0.8 pad_maximum_fusion
  120.2 3.5 %all-to-all-start.1 = ((f32[5,4,32,128]{3,2,0,1:T(8,128)}), f32[5,4,32,128]{3,2,0,1:T(8,128)S(1)}, u32[]{:S(2)}, u32[]{:S(2)}) async-start(f32[5,4,32,128]{3,2,0,1:T(8,128)} %pad_maximum_fusion), calls=%async_computation.1 | async-start | bytes 655360 | tf_op jit(solution)/shard_map/all_to_all | solution.py:71
  123.9 1.1 fusion.18
  125.0 5.4 %all-to-all-done.1 = f32[5,4,32,128]{3,2,0,1:T(8,128)S(1)} async-done(((f32[5,4,32,128]{3,2,0,1:T(8,128)}), f32[5,4,32,128]{3,2,0,1:T(8,128)S(1)}, u32[]{:S(2)}, u32[]{:S(2)}) %all-to-all-start.1) | async-done | bytes 327712 | tf_op jit(solution)/shard_map/all_to_all | solution.py:71
  130.4 0.6 fusion.38
  131.0 0.8 fusion.8
  131.8 0.6 slice_add_fusion.2
  (61 shorter events, 2.1 us)
Async XLA Ops:
  0.6 4.8 %copy-start.16 = (s32[8,16]{1,0:T(8,128)S(1)}, s32[8,16]{1,0:T(8,128)}, u32[]{:S(2)}) copy-start(s32[8,16]{1,0:T(8,128)} %param.10) | copy-start | bytes 1540
  8.7 7.4 %copy-start.5 = (f32[1,4,128,128]{3,2,1,0:T(8,128)S(1)}, f32[1,4,128,128]{3,2,1,0:T(8,128)}, u32[]{:S(2)}) copy-start(f32[1,4,128,128]{3,2,1,0:T(8,128)} %param.11) | copy-start | bytes 786436
  8.7 8.2 %copy-start.2 = (f32[2,4,128,128]{3,2,1,0:T(8,128)S(1)}, f32[2,4,128,128]{3,2,1,0:T(8,128)}, u32[]{:S(2)}) copy-start(f32[2,4,128,128]{3,2,1,0:T(8,128)} %param.14) | copy-start | bytes 1572868
  8.7 10.7 %copy-start.14 = (f32[1,32,128]{2,1,0:T(8,128)S(1)}, f32[1,32,128]{2,1,0:T(8,128)}, u32[]{:S(2)}) copy-start(f32[1,32,128]{2,1,0:T(8,128)} %param.12) | copy-start | bytes 49156
  8.7 10.7 %copy-start.15 = (f32[1,32,128]{2,1,0:T(8,128)S(1)}, f32[1,32,128]{2,1,0:T(8,128)}, u32[]{:S(2)}) copy-start(f32[1,32,128]{2,1,0:T(8,128)} %param.13) | copy-start | bytes 49156
  8.7 10.7 %copy-start.11 = (f32[2,32,128]{2,1,0:T(8,128)S(1)}, f32[2,32,128]{2,1,0:T(8,128)}, u32[]{:S(2)}) copy-start(f32[2,32,128]{2,1,0:T(8,128)} %param.15) | copy-start | bytes 98308
  8.7 10.8 %copy-start.12 = (f32[2,32,128]{2,1,0:T(8,128)S(1)}, f32[2,32,128]{2,1,0:T(8,128)}, u32[]{:S(2)}) copy-start(f32[2,32,128]{2,1,0:T(8,128)} %param.16) | copy-start | bytes 98308
  8.7 10.8 %copy-start.13 = (f32[2,32,128]{2,1,0:T(8,128)S(1)}, f32[2,32,128]{2,1,0:T(8,128)}, u32[]{:S(2)}) copy-start(f32[2,32,128]{2,1,0:T(8,128)} %param.17) | copy-start | bytes 98308
  8.7 100.7 %all-to-all-start = ((f32[8,4,2,128,128]{4,3,2,1,0:T(8,128)}), f32[8,4,2,128,128]{4,3,2,1,0:T(8,128)}, u32[]{:S(2)}, u32[]{:S(2)}) async-start(f32[8,4,2,128,128]{4,3,2,1,0:T(8,128)} %bitcast.131), calls=%async_computation | async-start | bytes 8388608 | tf_op jit(solution)/shard_map/all_to_all | solution.py:55
  17.6 24.5 %collective-permute-start = (f32[3,4,128,128]{3,2,1,0:T(8,128)}, f32[3,4,128,128]{3,2,1,0:T(8,128)S(1)}, u32[]{:S(2)}, u32[]{:S(2)}) collective-permute-start(f32[3,4,128,128]{3,2,1,0:T(8,128)} %constant_dynamic-update-slice_fusion), channel_id=1, source_target_pairs={{0,8},{8,16},{16,24},{24,0},{1,9},{9,17},{17,25},{25,1},{2,10},{10... | collective-permute-start | bytes 2359304 | tf_op jit(solution)/shard_map/ppermute | solution.py:47
  17.6 37.4 %collective-permute-start.2 = (f32[3,4,128,128]{3,2,1,0:T(8,128)}, f32[3,4,128,128]{3,2,1,0:T(8,128)S(1)}, u32[]{:S(2)}, u32[]{:S(2)}) collective-permute-start(f32[3,4,128,128]{3,2,1,0:T(8,128)} %constant_dynamic-update-slice_fusion), channel_id=1, source_target_pairs={{0,24},{8,0},{16,8},{24,16},{1,25},{9,1},{17,9},{25,17},{2,26},{10... | collective-permute-start | bytes 2359304 | tf_op jit(solution)/shard_map/ppermute | solution.py:50
  41.4 15.0 %copy-start = (f32[8,128,128]{2,1,0:T(8,128)}, f32[8,128,128]{2,1,0:T(8,128)S(1)}, u32[]{:S(2)}) copy-start(f32[8,128,128]{2,1,0:T(8,128)S(1)} %all_gather.3) | copy-start | bytes 1572868
  42.2 11.6 %collective-permute-start.1 = (f32[3,4,128,128]{3,2,1,0:T(8,128)S(1)}, f32[3,4,128,128]{3,2,1,0:T(8,128)}, u32[]{:S(2)}, u32[]{:S(2)}) collective-permute-start(f32[3,4,128,128]{3,2,1,0:T(8,128)S(1)} %collective-permute-done), channel_id=1, source_target_pairs={{0,8},{8,16},{16,24},{24,0},{1,9},{9,17},{17,25},{25,1},{2,10},{10... | collective-permute-start | bytes 2359304 | tf_op jit(solution)/shard_map/ppermute | solution.py:47
  42.8 13.7 %copy-start.9 = (f32[128,128]{1,0:T(8,128)}, f32[128,128]{1,0:T(8,128)S(1)}, u32[]{:S(2)}) copy-start(f32[128,128]{1,0:T(8,128)S(1)} %fusion.29) | copy-start | bytes 196612
  109.4 7.0 %copy-start.1 = (f32[8,128,128]{2,1,0:T(8,128)S(1)}, f32[8,128,128]{2,1,0:T(8,128)}, u32[]{:S(2)}) copy-start(f32[8,128,128]{2,1,0:T(8,128)} %copy-done) | copy-start | bytes 1572868
  109.4 8.1 %copy-start.3 = (f32[2,4,128,128]{2,3,1,0:T(8,128)S(1)}, f32[2,4,128,128]{2,3,1,0:T(8,128)}, u32[]{:S(2)}) copy-start(f32[2,4,128,128]{2,3,1,0:T(8,128)} %convolution_bitcast_fusion.1) | copy-start | bytes 1572868
  116.4 7.3 %copy-start.7 = (f32[128,2,128]{0,2,1:T(8,128)S(1)}, f32[128,2,128]{0,2,1:T(8,128)}, u32[]{:S(2)}) copy-start(f32[128,2,128]{0,2,1:T(8,128)} %fusion.24) | copy-start | bytes 393220
  116.4 7.5 %copy-start.8 = (f32[2,128,128]{1,2,0:T(8,128)S(1)}, f32[2,128,128]{1,2,0:T(8,128)}, u32[]{:S(2)}) copy-start(f32[2,128,128]{1,2,0:T(8,128)} %fusion.16) | copy-start | bytes 393220
  116.4 14.0 %copy-start.10 = (f32[128,128]{1,0:T(8,128)S(1)}, f32[128,128]{1,0:T(8,128)}, u32[]{:S(2)}) copy-start(f32[128,128]{1,0:T(8,128)} %copy-done.9) | copy-start | bytes 196612
  116.8 15.6 %copy-start.4 = (f32[4,128,128]{2,1,0:T(8,128)}, f32[4,128,128]{2,1,0:T(8,128)S(1)}, u32[]{:S(2)}) copy-start(f32[4,128,128]{2,1,0:T(8,128)S(1)} %convolution_negate_fusion.1) | copy-start | bytes 786436
  118.6 13.9 %copy-start.6 = (f32[2,4,128,128]{3,2,1,0:T(8,128)}, f32[2,4,128,128]{3,2,1,0:T(8,128)S(1)}, u32[]{:S(2)}) copy-start(f32[2,4,128,128]{3,2,1,0:T(8,128)S(1)} %convolution_negate_fusion) | copy-start | bytes 1572868
  120.2 10.2 %all-to-all-start.1 = ((f32[5,4,32,128]{3,2,0,1:T(8,128)}), f32[5,4,32,128]{3,2,0,1:T(8,128)S(1)}, u32[]{:S(2)}, u32[]{:S(2)}) async-start(f32[5,4,32,128]{3,2,0,1:T(8,128)} %pad_maximum_fusion), calls=%async_computation.1 | async-start | bytes 655360 | tf_op jit(solution)/shard_map/all_to_all | solution.py:71
